TPU v7x, 128 devices: a whole 4x4x4 slice. The times are simulated.
128 devices in a mesh: wide: 8 (over z, core), narrow: 16 (over x, y).
Axes of the slice: x: 4, y: 4, z: 4, core: 2. Of those that a mesh axis runs over, the one named last changes fastest.
Arguments:
- vectors: float32 [131072, 1024], P(('wide', 'narrow'))
- pivots: int32 [256], replicated, may hold values from 0 to 131071, as said below
- integrals: float32 [131072, 256], P(('wide', 'narrow')), as said below
- destination: int32 [131072], P(('wide', 'narrow')), may hold values from 0 to 131071, as said below
Outputs:
- new_vectors: float32 [131072, 256], P(('wide', 'narrow'))
Inputs may be any that keep to these rules, and one draw needn't show every extreme that they name: `pivots`: 256 distinct pair rows, the first and the last pair row among them. Every pair row is the destination of exactly one slot. Rows 1024 * d to 1024 * (d + 1) - 1 belong to the device of index d along wide+narrow; of the slots of one device, at most 16 belong to the rows of one device, and some device sends exactly 16 to some device. `integrals`: the pivot block of the residual is symmetric and positive definite.
All inputs are finite; a program needn't handle non-finite values.
Results may differ from a plain program's by a relative error of at most 0.000084.
Values sent between devices are 32-bit elements; how exact they have to be, the bound alone decides.
A program may use at most 64 MiB of HBM per device.

v0:
```python
import jax
import jax.numpy as jnp
from jax import lax
from jax.sharding import Mesh
from jax.sharding import PartitionSpec as P

ROWS_DEV = 1024
PIVOTS = 256
WIDE_NARROW = ("wide_0", "wide_1", "narrow_0", "narrow_1")
WIDE = ("wide_0", "wide_1")
NARROW = ("narrow_0", "narrow_1")


def in_blocks(shard, dim, peers):
    before, after = (shard.shape[:dim], shard.shape[dim + 1 :])
    return jnp.moveaxis(shard.reshape(*before, peers, -1, *after), dim, 0)


def joined_along(blocks, dim):
    blocks = jnp.moveaxis(blocks, 0, dim)
    lengths = blocks.shape
    return blocks.reshape(*lengths[:dim], lengths[dim] * lengths[dim + 1], *lengths[dim + 2 :])


def exchange_both(shard, axis, axes, splits, concats):
    sizes = [lax.axis_size(a) for a in axes]
    blocks = in_blocks(shard, splits[0], sizes[0])
    blocks = jnp.moveaxis(in_blocks(blocks, splits[1] + 1, sizes[1]), 0, 1)
    inside = blocks.shape[2:]
    blocks = blocks.reshape(-1, *inside)
    blocks = lax.all_to_all(blocks, axis, split_axis=0, concat_axis=0, tiled=True)
    blocks = joined_along(blocks.reshape(*sizes, *inside), concats[0] + 1)
    return joined_along(blocks, concats[1])


def rows_for(lines, peers):
    spare = -lines.shape[0] % peers
    if not spare:
        return lines
    return jnp.concatenate([lines, jnp.zeros((spare, *lines.shape[1:]), lines.dtype)])


def copy_for_each(shard, axis):
    peers = lax.axis_size(axis)
    return lax.all_to_all(
        jnp.broadcast_to(shard[None], (peers, *shard.shape)), axis, 0, 0, tiled=True
    )


def whole_of(shard, axes, dim):
    far, near = axes
    initial = copy_for_each(shard, far)
    blocks = jnp.swapaxes(copy_for_each(initial, near), 0, 1)
    return joined_along(blocks.reshape(-1, *shard.shape), dim)


def sum_at_owner(shard, axis, dim):
    peers = lax.axis_size(axis)
    blocks = lax.all_to_all(in_blocks(shard, dim, peers), axis, 0, 0, tiled=True)
    return jnp.sum(blocks, axis=0)


def sum_by_axis(shard, axes, dim):
    far, near = axes
    own = sum_at_owner(in_blocks(shard, dim, lax.axis_size(far)), near, dim + 1)
    return jnp.sum(lax.all_to_all(own, far, 0, 0, tiled=True), axis=0)


def sum_by_parts(shard, axes):
    padded = rows_for(shard, lax.axis_size(axes[0]) * lax.axis_size(axes[1]))
    whole = whole_of(sum_by_axis(padded, axes, 0), axes, 0)
    return lax.slice_in_dim(whole, 0, len(shard)).reshape(shard.shape)


def in_one(arrays, axis):
    ends = [0]
    for a in arrays:
        ends.append(ends[-1] + a.size)
    subtotal = sum_by_parts(jnp.concatenate([a.ravel() for a in arrays]), axis)
    return tuple((subtotal[b:e].reshape(a.shape) for a, b, e in zip(arrays, ends, ends[1:])))


def pick_local(source, row_index, is_mine):
    chosen = source[jnp.clip(row_index, 0, source.shape[0] - 1)]
    return jnp.where(is_mine[:, None], chosen, 0.0)


def shards(vectors, pivots, integrals, destination):
    devices = lax.axis_size(WIDE_NARROW)
    capacity = 2 * ROWS_DEV // devices
    first_row = lax.axis_index(WIDE_NARROW) * ROWS_DEV
    local_pivot = pivots - first_row
    is_mine = (local_pivot >= 0) & (local_pivot < ROWS_DEV)
    owner_index = destination // ROWS_DEV
    onehot = (owner_index[:, None] == jnp.arange(devices, dtype=jnp.int32)[None, :]).astype(
        jnp.int32
    )
    slot_rank = jnp.sum(jnp.cumsum(onehot, axis=0) * onehot, axis=1) - 1
    send_values = (
        jnp.zeros((devices, capacity, PIVOTS), jnp.float32)
        .at[owner_index, slot_rank]
        .set(integrals)
    )
    send_targets = (
        jnp.full((devices, capacity), ROWS_DEV, jnp.int32)
        .at[owner_index, slot_rank]
        .set(destination - owner_index * ROWS_DEV)
    )
    wide_count = lax.axis_size(WIDE)
    narrow_count = lax.axis_size(NARROW)
    received_values, received_targets = (
        exchange_both(
            send_values.reshape(wide_count, narrow_count, capacity, PIVOTS),
            WIDE_NARROW,
            (WIDE, NARROW),
            (0, 1),
            (0, 1),
        ),
        exchange_both(
            send_targets.reshape(wide_count, narrow_count, capacity),
            WIDE_NARROW,
            (WIDE, NARROW),
            (0, 1),
            (0, 1),
        ),
    )
    local_integrals = (
        jnp.zeros((ROWS_DEV, PIVOTS), jnp.float32)
        .at[received_targets.reshape(-1)]
        .set(received_values.reshape(-1, PIVOTS), mode="drop")
    )
    pivot_local = pick_local(vectors, local_pivot, is_mine)
    matches = destination[:, None] == pivots[None, :]
    pivot_slot = jnp.argmax(matches.astype(jnp.int32), axis=0)
    pivot_integrals = pick_local(integrals, pivot_slot, jnp.any(matches, axis=0))
    pivot_vecs, pivot_sums = in_one(
        (pivot_local, pivot_integrals), (("wide_0", "wide_1", "narrow_0"), "narrow_1")
    )
    residual = local_integrals - jnp.dot(
        vectors, pivot_vecs.T, precision=lax.Precision.HIGHEST, preferred_element_type=jnp.float32
    )
    pivot_block = pivot_sums - jnp.dot(
        pivot_vecs,
        pivot_vecs.T,
        precision=lax.Precision.HIGHEST,
        preferred_element_type=jnp.float32,
    )
    factor = jnp.linalg.cholesky(pivot_block)
    return jax.scipy.linalg.solve_triangular(factor, residual.T, lower=True).T


def solution(mesh):
    torus = Mesh(mesh.devices.reshape(4, 2, 4, 4), ("wide_0", "wide_1", "narrow_0", "narrow_1"))
    return jax.shard_map(
        shards,
        mesh=torus,
        in_specs=(P(WIDE_NARROW, None), P(), P(WIDE_NARROW, None), P(WIDE_NARROW)),
        out_specs=P(WIDE_NARROW, None),
        check_vma=False,
    )
```

profile of v0, /device:TPU:1, one launch (start us, length us, event | category | flops | bytes accessed | tf_op | source)
XLA Modules:
  0.0 214.7 jit_solution(12889867201187657088)
XLA Ops:
  0.0 1.7 fusion.2
  1.7 0.9 compare_reduce_fusion
  2.6 0.7 compare_select_fusion.4
  3.3 0.7 compare_and_fusion
  4.0 2.2 %gather_fusion.1 = f32[256,256]{1,0:T(8,128)S(1)} fusion(f32[1024,256]{1,0:T(8,128)} %param.6, s32[1024]{0:T(1024)S(1)} %pad_clamp_fusion), kind=kCustom, calls=%fused_computation.1 | custom fusion | bytes 525312 | tf_op jit(solution)/shard_map/gather | solution.py:84
  6.4 3.8 %gather_fusion = f32[256,1024]{1,0:T(8,128)S(1)} fusion(f32[1024,1024]{1,0:T(8,128)} %param.4, s32[1024]{0:T(1024)S(1)} %pad_clamp_fusion.1), kind=kCustom, calls=%fused_computation | custom fusion | bytes 2098176 | tf_op jit(solution)/shard_map/gather | solution.py:84
  10.7 0.5 reshape_reshape.10
  11.1 1.5 copy.46
  12.6 5.0 %all-to-all-start = ((f32[4,32,2560]{2,1,0:T(8,128)}), f32[4,32,2560]{2,1,0:T(8,128)S(1)}, u32[]{:S(2)}, u32[]{:S(2)}) async-start(f32[4,32,2560]{2,1,0:T(8,128)} %copy.46), calls=%async_computation | async-start | bytes 2621440 | tf_op jit(solution)/shard_map/all_to_all | solution.py:59
  18.7 16.0 %all-to-all-done = f32[4,32,2560]{2,1,0:T(8,128)S(1)} async-done(((f32[4,32,2560]{2,1,0:T(8,128)}), f32[4,32,2560]{2,1,0:T(8,128)S(1)}, u32[]{:S(2)}, u32[]{:S(2)}) %all-to-all-start) | async-done | bytes 1310752 | tf_op jit(solution)/shard_map/all_to_all | solution.py:59
  34.7 0.9 all_to_all.23
  35.7 9.7 %all-to-all-start.1 = ((f32[32,1,2560]{2,1,0:T(1,128)}), f32[32,1,2560]{2,1,0:T(1,128)S(1)}, u32[]{:S(2)}, u32[]{:S(2)}) async-start(f32[32,1,2560]{2,1,0:T(1,128)} %all_to_all.23), calls=%async_computation.1 | async-start | bytes 655360 | tf_op jit(solution)/shard_map/all_to_all | solution.py:66
  45.6 4.3 %scatter_custom_fusion.1 = s32[2048]{0:T(1024)S(1)} fusion(s32[1024]{0:T(1024)S(1)} %get-tuple-element.38, s32[1024]{0:T(1024)S(1)} %get-tuple-element.31, s32[]{:T(128)} %constant.134.clone.1), kind=kCustom, calls=%fused_computation.68 | custom fusion | bytes 8196
  49.9 0.7 copy.54
  50.6 4.4 %all-to-all-done.1 = f32[32,1,2560]{2,1,0:T(1,128)S(1)} async-done(((f32[32,1,2560]{2,1,0:T(1,128)}), f32[32,1,2560]{2,1,0:T(1,128)S(1)}, u32[]{:S(2)}, u32[]{:S(2)}) %all-to-all-start.1) | async-done | bytes 327712 | tf_op jit(solution)/shard_map/all_to_all | solution.py:66
  55.0 4.2 %all-to-all-start.4 = ((s32[128,1,1,16]{3,2,1,0:T(1,128)}), s32[128,1,1,16]{3,2,1,0:T(1,128)S(1)}, u32[]{:S(2)}, u32[]{:S(2)}) async-start(s32[128,1,1,16]{3,2,1,0:T(1,128)} %copy.54), calls=%async_computation.4 | async-start | bytes 131072 | tf_op jit(solution)/shard_map/all_to_all | solution.py:31
  59.4 9.4 %all-to-all-done.4 = s32[128,1,1,16]{3,2,1,0:T(1,128)S(1)} async-done(((s32[128,1,1,16]{3,2,1,0:T(1,128)}), s32[128,1,1,16]{3,2,1,0:T(1,128)S(1)}, u32[]{:S(2)}, u32[]{:S(2)}) %all-to-all-start.4) | async-done | bytes 8224 | tf_op jit(solution)/shard_map/all_to_all | solution.py:31
  68.8 0.9 broadcast_in_dim.74
  69.7 4.5 %all-to-all-start.2 = ((f32[32,1,2560]{2,1,0:T(1,128)}), f32[32,1,2560]{2,1,0:T(1,128)S(1)}, u32[]{:S(2)}, u32[]{:S(2)}) async-start(f32[32,1,2560]{2,1,0:T(1,128)} %broadcast_in_dim.74), calls=%async_computation.2 | async-start | bytes 655360 | tf_op jit(solution)/shard_map/all_to_all | solution.py:45
  74.2 6.7 %scatter_custom_fusion.2 = f32[2048,256]{1,0:T(8,128)} fusion(s32[1024]{0:T(1024)S(1)} %get-tuple-element.37, f32[1024,256]{1,0:T(8,128)} %param.6, f32[]{:T(128)} %constant.137.clone.1), kind=kCustom, calls=%fused_computation.18 | custom fusion | bytes 2097664
  80.8 2.9 %all-to-all-done.2 = f32[32,1,2560]{2,1,0:T(1,128)S(1)} async-done(((f32[32,1,2560]{2,1,0:T(1,128)}), f32[32,1,2560]{2,1,0:T(1,128)S(1)}, u32[]{:S(2)}, u32[]{:S(2)}) %all-to-all-start.2) | async-done | bytes 327712 | tf_op jit(solution)/shard_map/all_to_all | solution.py:45
  83.8 4.9 %all-to-all-start.5 = ((f32[128,1,1,16,256]{4,3,2,1,0:T(8,128)}), f32[128,1,1,16,256]{4,3,2,1,0:T(8,128)}, u32[]{:S(2)}, u32[]{:S(2)}) async-start(f32[128,1,1,16,256]{4,3,2,1,0:T(8,128)} %bitcast.22), calls=%async_computation.5 | async-start | bytes 4194304 | tf_op jit(solution)/shard_map/all_to_all | solution.py:31
  88.7 29.5 %all-to-all-done.5 = f32[128,1,1,16,256]{4,3,2,1,0:T(8,128)} async-done(((f32[128,1,1,16,256]{4,3,2,1,0:T(8,128)}), f32[128,1,1,16,256]{4,3,2,1,0:T(8,128)}, u32[]{:S(2)}, u32[]{:S(2)}) %all-to-all-start.5) | async-done | bytes 2097184 | tf_op jit(solution)/shard_map/all_to_all | solution.py:31
  118.1 1.2 broadcast_in_dim.76
  119.3 3.5 %all-to-all-start.3 = ((f32[4,32,2560]{2,1,0:T(8,128)}), f32[4,32,2560]{2,1,0:T(8,128)S(1)}, u32[]{:S(2)}, u32[]{:S(2)}) async-start(f32[4,32,2560]{2,1,0:T(8,128)} %broadcast_in_dim.76), calls=%async_computation.3 | async-start | bytes 2621440 | tf_op jit(solution)/shard_map/all_to_all | solution.py:45
  123.0 9.9 %scatter_custom_fusion = f32[1024,256]{1,0:T(8,128)S(1)} fusion(s32[2048]{0:T(1024)S(1)} %bitcast.106, f32[2048,256]{1,0:T(8,128)} %bitcast.27, f32[]{:T(128)} %constant.137.clone.1), kind=kCustom, calls=%fused_computation.31 | custom fusion | bytes 1049088 | tf_op jit(solution)/shard_map/scatter | solution.py:130
  132.9 1.3 copy.56
  134.2 5.5 %all-to-all-done.3 = f32[4,32,2560]{2,1,0:T(8,128)S(1)} async-done(((f32[4,32,2560]{2,1,0:T(8,128)}), f32[4,32,2560]{2,1,0:T(8,128)S(1)}, u32[]{:S(2)}, u32[]{:S(2)}) %all-to-all-start.3) | async-done | bytes 1310752 | tf_op jit(solution)/shard_map/all_to_all | solution.py:45
  139.7 0.8 copy.47
  140.6 0.7 slice.67
  141.3 1.7 slice.65
  142.9 1.0 slice.86
  144.1 1.0 convolution_subtract_fusion.1
  145.3 11.7 %cholesky.49 = f32[128,128]{1,0:T(8,128)S(1)} custom-call(f32[128,128]{1,0:T(8,128)S(1)} %cholesky.115), custom_call_target="Cholesky" | custom-call | tf_op jit(solution)/shard_map/jit(cholesky)/cholesky | solution.py:148
  157.1 6.2 %fusion.1 = f32[256,1024]{1,0:T(8,128)S(1)} fusion(f32[1024,256]{0,1:T(8,128)} %copy.56, f32[1024,1024]{1,0:T(8,128)} %param.4, f32[320,1024]{1,0:T(8,128)S(1)} %slice.67), kind=kOutput, calls=%fused_computation.9 | convolution fusion | flops 3221487616 | bytes 7340032 | tf_op jit(solution)/shard_map/dot_general | solution.py:139
  163.2 10.0 %custom-call.15 = f32[1,128,128]{1,2,0:T(8,128)S(1)} custom-call(f32[1,128,128]{2,1,0:T(8,128)S(1)} %get-tuple-element.30), custom_call_target="InvertDiagBlocksLowerTriangular" | custom-call | tf_op jit(solution)/shard_map/jit(cholesky)/cholesky | solution.py:148
  173.7 11.7 %cholesky.103 = f32[128,128]{1,0:T(8,128)S(1)} custom-call(f32[128,128]{1,0:T(8,128)S(1)} %convolution_subtract_fusion.2), custom_call_target="Cholesky" | custom-call | tf_op jit(solution)/shard_map/jit(cholesky)/cholesky | solution.py:148
  185.5 0.7 compare_reduce_fusion.1
  187.6 4.1 %while.1 = (s32[]{:T(128)}, f32[256,256]{1,0:T(8,128)S(1)}, s32[2,2]{1,0:T(2,128)S(1)}, f32[2,128,128]{2,1,0:T(8,128)S(1)}, s32[]{:T(128)}) while((s32[]{:T(128)}, f32[256,256]{1,0:T(8,128)S(1)}, s32[2,2]{1,0:T(2,128)S(1)}, f32[2,128,128]{2,1,0:T(8,128)S(1)}, s32[]{:T(128)}) %tuple.31), condition=%wide.while_cond, body=%wide.while_body.sunk | while | flops 2 | bytes 131189 | solution.py:149
  187.6 0.6 fusion.33
  188.2 1.4 bitcast_dynamic-update-slice_fusion.2
  189.7 0.6 fusion.33
  190.3 1.4 bitcast_dynamic-update-slice_fusion.2
  191.7 19.7 %custom-call.16 = f32[2,128,128]{1,2,0:T(8,128)S(1)} custom-call(f32[2,128,128]{2,1,0:T(8,128)S(1)} %get-tuple-element.14), custom_call_target="InvertDiagBlocksLowerTriangular" | custom-call | tf_op jit(solution)/shard_map/jit(_solve_triangular)/triangular_solve | solution.py:149
  211.4 0.6 fusion.7
  212.1 0.6 convolution_subtract_fusion
  212.6 0.6 fusion.17
  213.4 1.3 copy.57
  (51 shorter events, 3.3 us)
Async XLA Ops:
  11.1 6.5 %copy-start = (s32[1024]{0:T(1024)S(1)}, s32[1024]{0:T(1024)}, u32[]{:S(2)}) copy-start(s32[1024]{0:T(1024)} %param.7) | copy-start | bytes 12292
  12.6 22.1 %all-to-all-start = ((f32[4,32,2560]{2,1,0:T(8,128)}), f32[4,32,2560]{2,1,0:T(8,128)S(1)}, u32[]{:S(2)}, u32[]{:S(2)}) async-start(f32[4,32,2560]{2,1,0:T(8,128)} %copy.46), calls=%async_computation | async-start | bytes 2621440 | tf_op jit(solution)/shard_map/all_to_all | solution.py:59
  17.6 0.9 copy-start.2
  17.6 1.0 copy-start.3
  18.0 27.4 %copy-start.1 = (s32[2]{0:T(128)S(1)}, s32[2]{0:T(128)}, u32[]{:S(2)}) copy-start(s32[2]{0:T(128)} %constant.152) | copy-start | bytes 28
  35.7 19.3 %all-to-all-start.1 = ((f32[32,1,2560]{2,1,0:T(1,128)}), f32[32,1,2560]{2,1,0:T(1,128)S(1)}, u32[]{:S(2)}, u32[]{:S(2)}) async-start(f32[32,1,2560]{2,1,0:T(1,128)} %all_to_all.23), calls=%async_computation.1 | async-start | bytes 655360 | tf_op jit(solution)/shard_map/all_to_all | solution.py:66
  55.0 13.8 %all-to-all-start.4 = ((s32[128,1,1,16]{3,2,1,0:T(1,128)}), s32[128,1,1,16]{3,2,1,0:T(1,128)S(1)}, u32[]{:S(2)}, u32[]{:S(2)}) async-start(s32[128,1,1,16]{3,2,1,0:T(1,128)} %copy.54), calls=%async_computation.4 | async-start | bytes 131072 | tf_op jit(solution)/shard_map/all_to_all | solution.py:31
  69.7 14.1 %all-to-all-start.2 = ((f32[32,1,2560]{2,1,0:T(1,128)}), f32[32,1,2560]{2,1,0:T(1,128)S(1)}, u32[]{:S(2)}, u32[]{:S(2)}) async-start(f32[32,1,2560]{2,1,0:T(1,128)} %broadcast_in_dim.74), calls=%async_computation.2 | async-start | bytes 655360 | tf_op jit(solution)/shard_map/all_to_all | solution.py:45
  83.8 34.4 %all-to-all-start.5 = ((f32[128,1,1,16,256]{4,3,2,1,0:T(8,128)}), f32[128,1,1,16,256]{4,3,2,1,0:T(8,128)}, u32[]{:S(2)}, u32[]{:S(2)}) async-start(f32[128,1,1,16,256]{4,3,2,1,0:T(8,128)} %bitcast.22), calls=%async_computation.5 | async-start | bytes 4194304 | tf_op jit(solution)/shard_map/all_to_all | solution.py:31
  119.3 20.4 %all-to-all-start.3 = ((f32[4,32,2560]{2,1,0:T(8,128)}), f32[4,32,2560]{2,1,0:T(8,128)S(1)}, u32[]{:S(2)}, u32[]{:S(2)}) async-start(f32[4,32,2560]{2,1,0:T(8,128)} %broadcast_in_dim.76), calls=%async_computation.3 | async-start | bytes 2621440 | tf_op jit(solution)/shard_map/all_to_all | solution.py:45
where the time goes:
time: 216 us; the launch traced here: 215 us
  waiting for transfers between devices  67.7 us (31%)
  other arithmetic  59.5 us (28%)
  local copies, waits for them, and re-layouts  44.4 us (21%)
  starting transfers between devices  31.8 us (15%)
  matrix products  9.52 us (4%)
    all_to_all x2, waiting for transfers between devices, exchange_both(): lax.all_to_all(blocks, axis, split_axis=0, concat_axis=0, tiled=True)  38.9 us
    another operation x6, other arithmetic, shards(): factor = jnp.linalg.cholesky(pivot_block)  34.2 us
    another operation x3, other arithmetic, shards(): return jax.scipy.linalg.solve_triangular(factor, residual.T, lower=True).T  19.7 us
    all_to_all x1, waiting for transfers between devices, sum_at_owner(): lax.all_to_all(in_blocks(shard, dim, peers), axis, 0, 0, tiled=True)  16 us
    unnamed x14, local copies, waits for them, and re-layouts  11.5 us
    scatter x2, local copies, waits for them, and re-layouts, shards(): local_integrals = jnp.zeros((ROWS_DEV, PIVOTS), jnp.float32).at[received_...  11.2 us
    all_to_all x1, starting transfers between devices, sum_by_axis(): return jnp.sum(lax.all_to_all(own, far, 0, 0, tiled=True), axis=0)  9.74 us
    all_to_all x2, starting transfers between devices, exchange_both(): lax.all_to_all(blocks, axis, split_axis=0, concat_axis=0, tiled=True)  9.06 us
  transfers between devices with their start and end apart: 6, of which 6 were waited for; matrix products, arithmetic and copies ran while one was open for 11% of the time, Pallas kernels for 0%

commit v1 on v0

v1 whole, which is shorter than its diff:
```python
import jax, jax.numpy as jnp
from jax import lax
from jax.experimental import pallas as pl
from jax.experimental.pallas import tpu as pltpu
from jax.sharding import Mesh
from jax.sharding import PartitionSpec as P

F32, BF16, I32 = jnp.float32, jnp.bfloat16, jnp.int32
HI = lax.Precision.HIGHEST
NT = (((1,), (1,)), ((), ()))
NN = (((1,), (0,)), ((), ()))
BLOCK = 64
PAIRS = 131072
ROWS_DEV = 1024
VECS = 1024
PIVOTS = 256
CAP = 16


def dot_hi(a, b, dims=(((1,), (0,)), ((), ()))):
    return lax.dot_general(a, b, dims, precision=HI, preferred_element_type=F32)

def factor_block(s, at):
    rows = lax.broadcasted_iota(I32, (BLOCK, 2 * BLOCK), 0)
    lanes = lax.broadcasted_iota(I32, (BLOCK, 2 * BLOCK), 1)
    other = BLOCK - at
    inside = (lanes >= at) & (lanes < at + BLOCK)
    t = jnp.where(inside, s, (rows == lanes - other).astype(F32))
    done = []
    for j in range(0, BLOCK, 2):
        top = j // 8 * 8
        i = j - top
        r0, r1 = t[i : i + 1, :], t[i + 1 : i + 2, :]
        c0 = jnp.broadcast_to(t[:, at + j : at + j + 1], t.shape)
        c1 = jnp.broadcast_to(t[:, at + j + 1 : at + j + 2], t.shape)
        a, b, c = c0[i : i + 1, :], c0[i + 1 : i + 2, :], c1[i + 1 : i + 2, :]
        inv = 1.0 / (a * c - b * b)
        u0 = (c * inv) * r0 - (b * inv) * r1
        u1 = (a * inv) * r1 - (b * inv) * r0
        ia = 1.0 / a
        done.append(r0 * lax.rsqrt(a))
        done.append((r1 - (b * ia) * r0) * lax.rsqrt(c - b * (b * ia)))
        below = lax.broadcasted_iota(I32, t.shape, 0) > i + 1
        t = jnp.where(below, t - c0 * u0 - c1 * u1, t)
        if (j + 2) % 8 == 0:
            t = t[8:, :]
    full = jnp.concatenate(done, axis=0)
    return full[:, other : other + BLOCK]

def invert_factor(a_ref, w_ref):
    n = a_ref.shape[0]
    w_ref[...] = jnp.zeros_like(w_ref)
    for k in range(0, n, BLOCK):
        e = k + BLOCK
        base = k // 128 * 128
        inv = factor_block(a_ref[k:e, base : base + 128], k - base)
        if k == 0:
            wk = inv
        else:
            wk = jnp.concatenate([dot_hi(inv, w_ref[k:e, :k]), inv], axis=1)
        w_ref[k:e, :e] = wk
        if e < n:
            col = dot_hi(a_ref[e:, k:e], inv, NT)
            a_ref[e:, e:] = a_ref[e:, e:] - dot_hi(col, col, NT)
            w_ref[e:, :e] = w_ref[e:, :e] - dot_hi(col, wk)


WIDE_NARROW = ("wide_0", "wide_1", "narrow_0", "narrow_1")
WIDE = ("wide_0", "wide_1")
NARROW = ("narrow_0", "narrow_1")


def in_blocks(shard, dim, peers):
    before, after = (shard.shape[:dim], shard.shape[dim + 1 :])
    return jnp.moveaxis(shard.reshape(*before, peers, -1, *after), dim, 0)


def joined_along(blocks, dim):
    blocks = jnp.moveaxis(blocks, 0, dim)
    lengths = blocks.shape
    return blocks.reshape(*lengths[:dim], lengths[dim] * lengths[dim + 1], *lengths[dim + 2 :])


def exchange_both(shard, axis, axes, splits, concats):
    sizes = [lax.axis_size(a) for a in axes]
    blocks = in_blocks(shard, splits[0], sizes[0])
    blocks = jnp.moveaxis(in_blocks(blocks, splits[1] + 1, sizes[1]), 0, 1)
    inside = blocks.shape[2:]
    blocks = blocks.reshape(-1, *inside)
    blocks = lax.all_to_all(blocks, axis, split_axis=0, concat_axis=0, tiled=True)
    blocks = joined_along(blocks.reshape(*sizes, *inside), concats[0] + 1)
    return joined_along(blocks, concats[1])


def rows_for(lines, peers):
    spare = -lines.shape[0] % peers
    if not spare:
        return lines
    return jnp.concatenate([lines, jnp.zeros((spare, *lines.shape[1:]), lines.dtype)])


def copy_for_each(shard, axis):
    peers = lax.axis_size(axis)
    return lax.all_to_all(
        jnp.broadcast_to(shard[None], (peers, *shard.shape)), axis, 0, 0, tiled=True
    )


def whole_of(shard, axes, dim):
    far, near = axes
    initial = copy_for_each(shard, far)
    blocks = jnp.swapaxes(copy_for_each(initial, near), 0, 1)
    return joined_along(blocks.reshape(-1, *shard.shape), dim)


def sum_at_owner(shard, axis, dim):
    peers = lax.axis_size(axis)
    blocks = lax.all_to_all(in_blocks(shard, dim, peers), axis, 0, 0, tiled=True)
    return jnp.sum(blocks, axis=0)


def sum_by_axis(shard, axes, dim):
    far, near = axes
    own = sum_at_owner(in_blocks(shard, dim, lax.axis_size(far)), near, dim + 1)
    return jnp.sum(lax.all_to_all(own, far, 0, 0, tiled=True), axis=0)


def sum_by_parts(shard, axes):
    padded = rows_for(shard, lax.axis_size(axes[0]) * lax.axis_size(axes[1]))
    whole = whole_of(sum_by_axis(padded, axes, 0), axes, 0)
    return lax.slice_in_dim(whole, 0, len(shard)).reshape(shard.shape)


def in_one(arrays, axis):
    ends = [0]
    for a in arrays:
        ends.append(ends[-1] + a.size)
    subtotal = sum_by_parts(jnp.concatenate([a.ravel() for a in arrays]), axis)
    return tuple((subtotal[b:e].reshape(a.shape) for a, b, e in zip(arrays, ends, ends[1:])))


def split3(x):
    hi = x.astype(BF16)
    rest = x - hi.astype(F32)
    mid = rest.astype(BF16)
    return hi, mid, (rest - mid.astype(F32)).astype(BF16)


def dot_bf(a, b, dims=NN):
    return lax.dot_general(a, b, dims, preferred_element_type=F32)


def column(row):
    return jnp.broadcast_to(row.astype(F32), (128, row.shape[1])).T.astype(I32)


def prep_kernel(
    first_ref, piv_smem, piv_ref, dest_ref, ints_ref, vec_hbm,
    send_ref, tgt_ref, pivots_ref,
    place_ref, place_smem, vec_ref, sem, vec_sem,
):
    devices = PAIRS // ROWS_DEV
    load = pltpu.make_async_copy(vec_hbm, vec_ref, vec_sem)
    load.start()
    dest = dest_ref[...]
    owner = dest // ROWS_DEV
    local = dest - owner * ROWS_DEV
    onehot = lax.broadcasted_iota(I32, (devices, ROWS_DEV), 0) == owner
    onehot_bf = onehot.astype(F32).astype(BF16)
    before = (
        lax.broadcasted_iota(I32, (128, 128), 0) < lax.broadcasted_iota(I32, (128, 128), 1)
    ).astype(F32).astype(BF16)
    ranks = []
    carry = jnp.zeros((devices, 1), F32)
    for i in range(0, ROWS_DEV, 128):
        part = onehot_bf[:, i : i + 128]
        hot = onehot[:, i : i + 128]
        count = dot_bf(part, before) + carry
        ranks.append(jnp.sum(jnp.where(hot, count, 0.0), axis=0, keepdims=True))
        carry = carry + jnp.sum(hot.astype(F32), axis=1, keepdims=True)
    rank = jnp.concatenate(ranks, axis=1).astype(I32)
    place_ref[...] = owner * CAP + rank
    to_smem = pltpu.make_async_copy(place_ref, place_smem, sem)
    to_smem.start()
    hit = lax.broadcasted_iota(I32, (CAP, ROWS_DEV), 0) == rank
    local1 = local + 1
    high = jnp.where(hit, local1 // 32, 0).astype(F32).astype(BF16)
    low = jnp.where(hit, local1 % 32, 0).astype(F32).astype(BF16)
    tgt_ref[...] = (dot_bf(onehot_bf, high, NT) * 32.0 + dot_bf(onehot_bf, low, NT)).astype(I32)

    piv_col = column(piv_ref[...])
    match = jnp.concatenate(
        [piv_col == dest[:, i : i + 128] for i in range(0, ROWS_DEV, 128)], axis=1
    ).astype(F32).astype(BF16)
    pivots_ref[:, VECS:] = sum(dot_bf(match, part) for part in split3(ints_ref[...]))

    to_smem.wait()

    def put(t, _):
        s = pl.multiple_of(t * 8, 8)
        for u in range(8):
            send_ref[pl.ds(place_smem[0, s + u], 1), :] = ints_ref[pl.ds(s + u, 1), :]
        return 0

    lax.fori_loop(0, ROWS_DEV // 8, put, 0)
    load.wait()
    pivots_ref[:, :VECS] = jnp.zeros((PIVOTS, VECS), F32)
    first = first_ref[0]

    def pick(j, _):
        row = piv_smem[j] - first

        @pl.when((row >= 0) & (row < ROWS_DEV))
        def _():
            pivots_ref[pl.ds(j, 1), :VECS] = vec_ref[pl.ds(row, 1), :]

        return 0

    lax.fori_loop(0, PIVOTS, pick, 0, unroll=4)


def prepare(vectors, pivots, integrals, destination, first_row):
    devices = PAIRS // ROWS_DEV
    vmem = pl.BlockSpec(memory_space=pltpu.VMEM)
    smem = pl.BlockSpec(memory_space=pltpu.SMEM)
    return pl.pallas_call(
        prep_kernel,
        out_shape=(
            jax.ShapeDtypeStruct((devices * CAP, PIVOTS), F32),
            jax.ShapeDtypeStruct((devices, CAP), I32),
            jax.ShapeDtypeStruct((PIVOTS, VECS + PIVOTS), F32),
        ),
        in_specs=[smem, smem, vmem, vmem, vmem, pl.BlockSpec(memory_space=pl.ANY)],
        out_specs=(vmem, vmem, vmem),
        scratch_shapes=[
            pltpu.VMEM((1, ROWS_DEV), I32),
            pltpu.SMEM((1, ROWS_DEV), I32),
            pltpu.VMEM((ROWS_DEV, VECS), F32),
            pltpu.SemaphoreType.DMA,
            pltpu.SemaphoreType.DMA,
        ],
        name="prepare",
    )(first_row.reshape(1), pivots, pivots.reshape(1, -1), destination.reshape(1, -1), integrals, vectors)


def factor_kernel(piv_ref, w_ref, a_ref):
    vecs = piv_ref[:, :VECS]
    block = piv_ref[:, VECS:] - dot_hi(vecs, vecs, NT)
    a_ref[...] = (block + block.T) * 0.5
    invert_factor(a_ref, w_ref)


def factor(pivot_rows):
    return pl.pallas_call(
        factor_kernel,
        out_shape=jax.ShapeDtypeStruct((PIVOTS, PIVOTS), F32),
        scratch_shapes=[pltpu.VMEM((PIVOTS, PIVOTS), F32)],
        name="factor",
    )(pivot_rows)


def dot3(a, b, dims):
    ah = a.astype(BF16)
    al = (a - ah.astype(F32)).astype(BF16)
    bh = b.astype(BF16)
    bl = (b - bh.astype(F32)).astype(BF16)
    return dot_bf(ah, bh, dims) + (dot_bf(ah, bl, dims) + dot_bf(al, bh, dims))


def finish_kernel(tgt_smem, recv_ref, vec_ref, piv_ref, w_ref, out_ref, rows_ref):
    devices = PAIRS // ROWS_DEV
    product = dot3(vec_ref[...], piv_ref[...], NT)

    def take(d, _):
        for k in range(CAP):
            rows_ref[pl.ds(tgt_smem[d, k], 1), :] = recv_ref[pl.ds(d * CAP + k, 1), :]
        return 0

    lax.fori_loop(0, devices, take, 0)
    out_ref[...] = dot3(rows_ref[1 : ROWS_DEV + 1, :] - product, w_ref[...], NT)


def finish(targets, received, vectors, pivot_vecs, inverse):
    vmem = pl.BlockSpec(memory_space=pltpu.VMEM)
    return pl.pallas_call(
        finish_kernel,
        out_shape=jax.ShapeDtypeStruct((ROWS_DEV, PIVOTS), F32),
        in_specs=[pl.BlockSpec(memory_space=pltpu.SMEM)] + [vmem] * 4,
        out_specs=vmem,
        scratch_shapes=[pltpu.VMEM((ROWS_DEV + 8, PIVOTS), F32)],
        name="finish",
    )(targets, received, vectors, pivot_vecs, inverse)


def shards(vectors, pivots, integrals, destination):
    first_row = lax.axis_index(WIDE_NARROW) * ROWS_DEV
    send_values, send_targets, own_pivots = prepare(vectors, pivots, integrals, destination, first_row)
    wide_count = lax.axis_size(WIDE)
    narrow_count = lax.axis_size(NARROW)
    values, targets = (
        exchange_both(
            send_values.reshape(wide_count, narrow_count, CAP, PIVOTS),
            WIDE_NARROW, (WIDE, NARROW), (0, 1), (0, 1),
        ),
        exchange_both(
            send_targets.reshape(wide_count, narrow_count, CAP),
            WIDE_NARROW, (WIDE, NARROW), (0, 1), (0, 1),
        ),
    )
    (pivot_rows,) = in_one((own_pivots,), (("wide_0", "wide_1", "narrow_0"), "narrow_1"))
    inverse = factor(pivot_rows)
    targets = targets.reshape(wide_count * narrow_count, CAP)
    return finish(targets, values.reshape(-1, PIVOTS), vectors, pivot_rows[:, :VECS], inverse)


def solution(mesh):
    torus = Mesh(mesh.devices.reshape(4, 2, 4, 4), ("wide_0", "wide_1", "narrow_0", "narrow_1"))
    return jax.shard_map(
        shards,
        mesh=torus,
        in_specs=(P(WIDE_NARROW, None), P(), P(WIDE_NARROW, None), P(WIDE_NARROW)),
        out_specs=P(WIDE_NARROW, None),
        check_vma=False,
    )
```

time: 216 us -> 154 us (0.71)
  blocking collectives: 0 us -> 73.8 us
  other arithmetic: 59.5 us -> 0.29 us
  waiting for transfers between devices: 67.7 us -> 14.9 us
  Pallas kernels: 0 us -> 44.1 us
  local copies, waits for them, and re-layouts: 44.4 us -> 9.99 us
  starting transfers between devices: 31.8 us -> 9.86 us
  matrix products: 9.52 us -> 0 us
    all_to_all x0 -> x4, blocking collectives: none -> 73.8 us  [the longest x2 32.9 us: copy_for_each(): lax.all_to_all(jnp.broadcast_to(shard[None], (peers, *shard.shape)), axis...]
    another operation x13 -> x0, other arithmetic: 55.8 us -> none  [the longest x6 34.2 us: shards(): factor = jnp.linalg.cholesky(pivot_block)]
    pallas_call x0 -> x3, Pallas kernels: none -> 44.1 us  [the longest x1 18.6 us: factor(): pl.pallas_call(factor_kernel, out_shape=jax.ShapeDtypeStruct((PIVOTS, PIV...]
    all_to_all x4 -> x0, waiting for transfers between devices: 28.8 us -> none  [the longest x1 16 us: sum_at_owner(): lax.all_to_all(in_blocks(shard, dim, peers), axis, 0, 0, tiled=True)]
    all_to_all x2, waiting for transfers between devices: 38.9 us -> 14.9 us  [exchange_both(): lax.all_to_all(blocks, axis, split_axis=0, concat_axis=0, tiled=True)]
    all_to_all x4 -> x0, starting transfers between devices: 22.8 us -> none  [the longest x1 9.74 us: sum_by_axis(): return jnp.sum(lax.all_to_all(own, far, 0, 0, tiled=True), axis=0)]
    scatter x2 -> x0, local copies, waits for them, and re-layouts: 11.2 us -> none  [shards(): local_integrals = jnp.zeros((ROWS_DEV, PIVOTS), jnp.float32).at[received_...]
    unnamed x14 -> x7, local copies, waits for them, and re-layouts: 11.5 us -> 1.37 us
  transfers between devices with their start and end apart: 6 -> 2, of which waited for: 6 -> 2; matrix products, arithmetic and copies ran while one was open for 11% -> 4% of each run, Pallas kernels for 0% -> 12%
where the time goes in v1:
time: 154 us; the launch traced here: 153 us
  blocking collectives  73.8 us (48%)
  Pallas kernels  44.1 us (29%)
  waiting for transfers between devices  14.9 us (10%)
  local copies, waits for them, and re-layouts  9.99 us (6%)
  starting transfers between devices  9.86 us (6%)
    all_to_all x2, blocking collectives, copy_for_each(): lax.all_to_all(jnp.broadcast_to(shard[None], (peers, *shard.shape)), axis...  32.9 us
    all_to_all x1, blocking collectives, sum_at_owner(): lax.all_to_all(in_blocks(shard, dim, peers), axis, 0, 0, tiled=True)  21.8 us
    all_to_all x1, blocking collectives, sum_by_axis(): return jnp.sum(lax.all_to_all(own, far, 0, 0, tiled=True), axis=0)  19.1 us
    pallas_call x1, Pallas kernels, factor(): pl.pallas_call(factor_kernel, out_shape=jax.ShapeDtypeStruct((PIVOTS, PIV...  18.6 us
    pallas_call x1, Pallas kernels, finish(): pl.pallas_call(finish_kernel, out_shape=jax.ShapeDtypeStruct((ROWS_DEV, P...  14.9 us
    all_to_all x2, waiting for transfers between devices, exchange_both(): lax.all_to_all(blocks, axis, split_axis=0, concat_axis=0, tiled=True)  14.9 us
    pallas_call x1, Pallas kernels, prepare(): pl.pallas_call(prep_kernel, out_shape=(jax.ShapeDtypeStruct((devices * CA...  10.6 us
    all_to_all x2, starting transfers between devices, exchange_both(): lax.all_to_all(blocks, axis, split_axis=0, concat_axis=0, tiled=True)  9.86 us
  transfers between devices with their start and end apart: 2, of which 2 were waited for; matrix products, arithmetic and copies ran while one was open for 4% of the time, Pallas kernels for 12%

profile of v1, /device:TPU:1, one launch (start us, length us, event | category | flops | bytes accessed | tf_op | source)
XLA Modules:
  0.0 153.1 jit_solution(7855940885891425354)
XLA Ops:
  0.0 10.6 %prepare.1 = (f32[2048,256]{1,0:T(8,128)}, s32[128,16]{1,0:T(8,128)}, f32[256,1280]{1,0:T(8,128)}) custom-call(s32[1]{0:T(128)} %bitcast.first_ref, s32[256]{0:T(256)} %piv_smem.1, s32[1,256]{1,0:T(1,128)} %bitcast.40, s32[1,1024]{1,0:T(1,128)} %bitcast.41, f32[1024,256]{1,0:T(8,128)} %ints_ref.1, f32[1024,1024]{1,0:T(8,128)} %vec_ref.1), custom_call_target="tpu_custom_call" | custom-call | tf_op jit(solution)/shard_map/prepare/pallas_call | solution.py:226
  10.6 1.9 %reshape_reshape_reshape.6 = f32[32,4,2560]{2,1,0:T(4,128)S(1)} reshape(f32[256,1280]{1,0:T(8,128)} %get-tuple-element.10) | data formatting | bytes 2621440 | tf_op jit(solution)/shard_map/reshape;reshape;reshape | solution.py:75
  12.5 0.4 copy.12
  13.0 21.8 %all_to_all.35 = f32[4,32,2560]{2,1,0:T(8,128)S(1)} all-to-all(f32[4,32,2560]{2,1,0:T(8,128)S(1)} %bitcast.36), channel_id=1, replica_groups=mesh['wide_0'=4,'wide_1'=2,'narrow_0'=4,'narrow_1'=4] {'narrow_1'}, dimensions={0} | all-to-all | bytes 2621440 | tf_op jit(solution)/shard_map/all_to_all | solution.py:118
  34.8 0.1 reduce_sum.18
  34.9 0.2 all_to_all.25
  35.1 19.1 %all_to_all.36 = f32[32,1,2560]{2,1,0:T(1,128)S(1)} all-to-all(f32[32,1,2560]{2,1,0:T(1,128)S(1)} %all_to_all.25), channel_id=1, replica_groups=mesh['wide_0'=4,'wide_1'=2,'narrow_0'=4,'narrow_1'=4] {'wide_0','wide_1'..., dimensions={0} | all-to-all | bytes 655360 | tf_op jit(solution)/shard_map/all_to_all | solution.py:125
  54.2 0.2 reduce_sum.19
  54.4 0.2 broadcast_in_dim.6
  54.6 13.5 %all_to_all.37 = f32[32,1,2560]{2,1,0:T(1,128)S(1)} all-to-all(f32[32,1,2560]{2,1,0:T(1,128)S(1)} %broadcast_in_dim.6), channel_id=1, replica_groups=mesh['wide_0'=4,'wide_1'=2,'narrow_0'=4,'narrow_1'=4] {'wide_0','wide_1'..., dimensions={0} | all-to-all | bytes 655360 | tf_op jit(solution)/shard_map/all_to_all | solution.py:104
  68.1 4.2 %all-to-all-start = ((s32[128,1,1,16]{3,2,1,0:T(1,128)}), s32[128,1,1,16]{3,2,1,0:T(1,128)S(1)}, u32[]{:S(2)}, u32[]{:S(2)}) async-start(s32[128,1,1,16]{3,2,1,0:T(1,128)} %bitcast.4), calls=%async_computation | async-start | bytes 131072 | tf_op jit(solution)/shard_map/all_to_all | solution.py:90
  72.3 9.5 %all-to-all-done = s32[128,1,1,16]{3,2,1,0:T(1,128)S(1)} async-done(((s32[128,1,1,16]{3,2,1,0:T(1,128)}), s32[128,1,1,16]{3,2,1,0:T(1,128)S(1)}, u32[]{:S(2)}, u32[]{:S(2)}) %all-to-all-start) | async-done | bytes 8224 | tf_op jit(solution)/shard_map/all_to_all | solution.py:90
  81.8 0.0 copy-start.2
  81.8 0.1 broadcast_in_dim.16
  81.9 19.5 %all_to_all.38 = f32[4,32,2560]{2,1,0:T(8,128)S(1)} all-to-all(f32[4,32,2560]{2,1,0:T(8,128)S(1)} %broadcast_in_dim.16), channel_id=1, replica_groups=mesh['wide_0'=4,'wide_1'=2,'narrow_0'=4,'narrow_1'=4] {'narrow_1'}, dimensions={0} | all-to-all | bytes 2621440 | tf_op jit(solution)/shard_map/all_to_all | solution.py:104
  101.4 0.0 copy-done.2
  101.4 5.7 %all-to-all-start.1 = ((f32[128,1,1,16,256]{4,3,2,1,0:T(8,128)}), f32[128,1,1,16,256]{4,3,2,1,0:T(8,128)S(1)}, u32[]{:S(2)}, u32[]{:S(2)}) async-start(f32[128,1,1,16,256]{4,3,2,1,0:T(8,128)} %bitcast.37), calls=%async_computation.1 | async-start | bytes 4194304 | tf_op jit(solution)/shard_map/all_to_all | solution.py:90
  107.1 1.9 %copy.8 = f32[32,4,2560]{2,1,0:T(4,128)} copy(f32[32,4,2560]{2,0,1:T(8,128)S(1)} %bitcast.35) | data formatting | bytes 2621440 | tf_op jit(solution)/shard_map/transpose | solution.py:112
  109.0 2.7 %reshape_reshape_reshape.7.piv_ref = f32[256,1280]{1,0:T(8,128)} reshape(f32[32,4,2560]{2,1,0:T(4,128)} %copy.8) | data formatting | bytes 2621440 | tf_op jit(solution)/shard_map/reshape;reshape;reshape | solution.py:139
  111.7 0.0 copy-start
  111.7 18.6 %factor.1.w_ref = f32[256,256]{1,0:T(8,128)} custom-call(f32[256,1280]{1,0:T(8,128)} %reshape_reshape_reshape.7.piv_ref), custom_call_target="tpu_custom_call" | custom-call | tf_op jit(solution)/shard_map/factor/pallas_call | solution.py:254
  130.2 0.0 copy-done
  130.2 1.1 slice.4.piv_ref
  131.4 5.4 %all-to-all-done.1 = f32[128,1,1,16,256]{4,3,2,1,0:T(8,128)S(1)} async-done(((f32[128,1,1,16,256]{4,3,2,1,0:T(8,128)}), f32[128,1,1,16,256]{4,3,2,1,0:T(8,128)S(1)}, u32[]{:S(2)}, u32[]{:S(2)}) %all-to-all-start.1) | async-done | bytes 2097184 | tf_op jit(solution)/shard_map/all_to_all | solution.py:90
  136.8 0.0 copy-start.1
  136.8 1.3 copy-done.1
  138.1 14.9 %finish.1 = f32[1024,256]{1,0:T(8,128)} custom-call(s32[128,16]{1,0:T(8,128)} %bitcast.39, f32[2048,256]{1,0:T(8,128)} %bitcast.34, f32[1024,1024]{1,0:T(8,128)} %vec_ref.1, f32[256,1024]{1,0:T(8,128)} %slice.4.piv_ref, f32[256,256]{1,0:T(8,128)} %factor.1.w_ref), custom_call_target="tpu_custom_call" | custom-call | tf_op jit(solution)/shard_map/finish/pallas_call | solution.py:285
  (1 shorter events, 0.0 us)
Async XLA Ops:
  68.1 13.7 %all-to-all-start = ((s32[128,1,1,16]{3,2,1,0:T(1,128)}), s32[128,1,1,16]{3,2,1,0:T(1,128)S(1)}, u32[]{:S(2)}, u32[]{:S(2)}) async-start(s32[128,1,1,16]{3,2,1,0:T(1,128)} %bitcast.4), calls=%async_computation | async-start | bytes 131072 | tf_op jit(solution)/shard_map/all_to_all | solution.py:90
  81.8 19.6 %copy-start.2 = (s32[128,1,1,16]{3,2,1,0:T(1,128)}, s32[128,1,1,16]{3,2,1,0:T(1,128)S(1)}, u32[]{:S(2)}) copy-start(s32[128,1,1,16]{3,2,1,0:T(1,128)S(1)} %all-to-all-done) | copy-start | bytes 24580
  101.4 35.4 %all-to-all-start.1 = ((f32[128,1,1,16,256]{4,3,2,1,0:T(8,128)}), f32[128,1,1,16,256]{4,3,2,1,0:T(8,128)S(1)}, u32[]{:S(2)}, u32[]{:S(2)}) async-start(f32[128,1,1,16,256]{4,3,2,1,0:T(8,128)} %bitcast.37), calls=%async_computation.1 | async-start | bytes 4194304 | tf_op jit(solution)/shard_map/all_to_all | solution.py:90
  111.7 18.6 %copy-start = (f32[256,1280]{1,0:T(8,128)S(1)}, f32[256,1280]{1,0:T(8,128)}, u32[]{:S(2)}) copy-start(f32[256,1280]{1,0:T(8,128)} %reshape_reshape_reshape.7.piv_ref) | copy-start | bytes 3932164
  136.8 1.3 copy-start.1
